TPU v7x, 32 devices: a whole 2x2x4 slice. The times are simulated.
32 devices in a mesh: dp: 4 (over x, core), mp: 8 (over z, y).
Axes of the slice: x: 2, y: 2, z: 4, core: 2. Of those that a mesh axis runs over, the one named last changes fastest.
Arguments:
- tokens: bfloat16 [32768, 768], P(('dp', 'mp')), may hold values from -6 to 6
- lengths: int32 [64], P(('dp', 'mp')), may hold values from 16 to 512, as said below
- w_in: bfloat16 [768, 3072], P('dp', 'mp'), may hold values from -0.21875 to 0.21875
- b_in: bfloat16 [3072], P('mp'), may hold values from -3 to 3
- w_out: bfloat16 [3072, 768], P('mp', 'dp'), may hold values from -0.109375 to 0.109375
- b_out: float32 [768], replicated, may hold values from -2 to 2
- gain_mix: float32 [768], replicated, may hold values from 0.25 to 1.75
- shift_mix: float32 [768], replicated, may hold values from -2 to 2
- gain_ffn: float32 [768], replicated, may hold values from 0.25 to 1.75
- shift_ffn: float32 [768], replicated, may hold values from -2 to 2
- cotangent: bfloat16 [32768, 768], P(('dp', 'mp')), may hold values from -6 to 6
Outputs:
- layer_out: bfloat16 [32768, 768], P(('dp', 'mp'))
- grad_tokens: bfloat16 [32768, 768], P(('dp', 'mp'))
- grad_w_in: float32 [768, 3072], P('dp', 'mp')
- grad_b_in: float32 [3072], replicated
- grad_w_out: float32 [3072, 768], P('mp', 'dp')
- grad_b_out: float32 [768], replicated
- grad_gain_mix: float32 [768], replicated
- grad_shift_mix: float32 [768], replicated
- grad_gain_ffn: float32 [768], replicated
- grad_shift_ffn: float32 [768], replicated
Inputs may be any that keep to these rules, and one draw needn't show every extreme that they name: `lengths`: in every aligned block of 8 items exactly one has length 512; the others have at most 256.
All inputs are finite; a program needn't handle non-finite values.
Results may differ from a plain program's by a relative error of at most 0.0095.
Values may be sent and summed in bfloat16 or wider, within the bound.
No kernel may reach another device: no remote copies, remote signals or barrier semaphores. Data moves between devices by JAX's collectives and lax.ppermute only.
A program may use at most 320 MiB of HBM per device.

v0:
```python
from functools import partial
import math
import jax
import jax.numpy as jnp
from jax import lax
from jax.sharding import PartitionSpec as P

D = 768
FF = 3072
LEN = 512
MB = 2
SEQ_MB = 1
epsilon = 1e-06


def dft_tables(width):
    index = jnp.arange(width, dtype=jnp.int32)
    phase = index[:, None] * index[None, :] % width
    angle = phase.astype(jnp.float32) * (2.0 * math.pi / width)
    factor = 1.0 / math.sqrt(width)
    return (jnp.cos(angle) * factor, jnp.sin(angle) * factor)


def layer_norm(values, gain, shift):
    center = values - jnp.mean(values, axis=-1, keepdims=True)
    spread = jnp.mean(center * center, axis=-1, keepdims=True)
    return center * lax.rsqrt(spread + epsilon) * gain + shift


def masked_norm(values, gain, shift, live_mask):
    return live_mask * layer_norm(values, gain, shift)


def inner_rows(left, right):
    return lax.dot_general(
        left, right, (((1,), (1,)), ((), ())), preferred_element_type=jnp.float32
    )


def outer_rows(left, right):
    return lax.dot_general(
        left, right, (((0,), (0,)), ((), ())), preferred_element_type=jnp.float32
    )


def body(
    tokens, lengths, w_in, b_in, w_out, b_out, gain_mix, shift_mix, gain_ffn, shift_ffn, cotangent
):
    ff_local = w_in.shape[1]
    tok_rows = SEQ_MB * LEN
    cos_feat, sin_feat = dft_tables(D)
    feat_table = jnp.concatenate([cos_feat, sin_feat], axis=1).astype(jnp.bfloat16)
    cos_seq, sin_seq = dft_tables(LEN)
    seq_table = jnp.concatenate([cos_seq, -sin_seq], axis=1).astype(jnp.bfloat16)
    w_out_turned = w_out.T
    grad_w_in = jnp.zeros((D, ff_local), jnp.float32)
    grad_w_turned = jnp.zeros((D, ff_local), jnp.float32)
    grad_b_in = jnp.zeros((ff_local,), jnp.float32)
    grad_b_out = jnp.zeros((D,), jnp.float32)
    grad_gain_mix = jnp.zeros((D,), jnp.float32)
    grad_shift_mix = jnp.zeros((D,), jnp.float32)
    grad_gain_ffn = jnp.zeros((D,), jnp.float32)
    grad_shift_ffn = jnp.zeros((D,), jnp.float32)
    positions = jnp.arange(LEN, dtype=jnp.int32)
    outputs = []
    input_grads = []
    for micro in range(MB):
        inputs = lax.slice_in_dim(tokens, micro * tok_rows, (micro + 1) * tok_rows, axis=0)
        cot_part = lax.slice_in_dim(cotangent, micro * tok_rows, (micro + 1) * tok_rows, axis=0)
        item_lengths = lax.slice_in_dim(lengths, micro * SEQ_MB, (micro + 1) * SEQ_MB, axis=0)
        live_mask = (
            (positions[None, :] < item_lengths[:, None]).astype(jnp.float32).reshape(tok_rows, 1)
        )
        masked = inputs * live_mask.astype(jnp.bfloat16)
        spectra = jnp.dot(masked, feat_table, preferred_element_type=jnp.float32).astype(
            jnp.bfloat16
        )
        stacked = (
            spectra.reshape(SEQ_MB, LEN, 2, D).transpose(0, 2, 1, 3).reshape(SEQ_MB, 2 * LEN, D)
        )
        mixed = jnp.einsum(
            "st,gtd->gsd", seq_table, stacked, preferred_element_type=jnp.float32
        ).reshape(tok_rows, D)
        first, first_back = jax.vjp(
            layer_norm, masked.astype(jnp.float32) + mixed, gain_mix, shift_mix
        )
        first_low = first.astype(jnp.bfloat16)
        w_in_rows, w_out_rows = (
            lax.all_gather(w_in, "dp", axis=0, tiled=True),
            lax.all_gather(w_out_turned, "dp", axis=0, tiled=True),
        )
        gathered = lax.all_gather(first_low, "mp", axis=0, tiled=True)
        pre_act = jnp.dot(gathered, w_in_rows, preferred_element_type=jnp.float32) + b_in.astype(
            jnp.float32
        )
        activation, gelu_back = jax.vjp(jax.nn.gelu, pre_act)
        hidden = activation.astype(jnp.bfloat16)
        branch = (
            lax.psum_scatter(inner_rows(hidden, w_out_rows), "mp", scatter_dimension=0, tiled=True)
            + b_out
        )
        result, last_back = jax.vjp(
            partial(masked_norm, live_mask=live_mask), first + branch, gain_ffn, shift_ffn
        )
        outputs.append(result.astype(jnp.bfloat16))
        grad_second, gain_part, shift_part = last_back(cot_part.astype(jnp.float32))
        grad_gain_ffn = grad_gain_ffn + gain_part
        grad_shift_ffn = grad_shift_ffn + shift_part
        grad_branch = grad_second.astype(jnp.bfloat16)
        grad_b_out = grad_b_out + jnp.sum(grad_branch.astype(jnp.float32), axis=0)
        grad_gathered = lax.all_gather(grad_branch, "mp", axis=0, tiled=True)
        grad_hidden = jnp.dot(grad_gathered, w_out_rows, preferred_element_type=jnp.float32)
        grad_pre = gelu_back(grad_hidden)[0].astype(jnp.bfloat16)
        grad_b_in = grad_b_in + jnp.sum(grad_pre.astype(jnp.float32), axis=0)
        grad_w_in = grad_w_in + outer_rows(gathered, grad_pre)
        grad_w_turned = grad_w_turned + outer_rows(grad_gathered, hidden)
        grad_ffn = lax.psum_scatter(
            inner_rows(grad_pre, w_in_rows), "mp", scatter_dimension=0, tiled=True
        )
        grad_sum, gain_part, shift_part = first_back(grad_second + grad_ffn)
        grad_gain_mix = grad_gain_mix + gain_part
        grad_shift_mix = grad_shift_mix + shift_part
        grad_mixed = grad_sum.astype(jnp.bfloat16).reshape(SEQ_MB, LEN, D)
        grad_stack = jnp.einsum(
            "st,gsd->gtd", seq_table, grad_mixed, preferred_element_type=jnp.float32
        ).astype(jnp.bfloat16)
        grad_spectra = (
            grad_stack.reshape(SEQ_MB, 2, LEN, D).transpose(0, 2, 1, 3).reshape(tok_rows, 2 * D)
        )
        grad_masked = grad_sum + inner_rows(grad_spectra, feat_table)
        input_grads.append((grad_masked * live_mask).astype(jnp.bfloat16))
    offset = lax.axis_index("mp") * ff_local
    bias_grad_full = lax.dynamic_update_slice(jnp.zeros((FF,), jnp.float32), grad_b_in, (offset,))
    grad_w_in_part, grad_w_turned_part = (
        lax.psum_scatter(
            grad_w_in.astype(jnp.bfloat16), "dp", scatter_dimension=0, tiled=True
        ).astype(jnp.float32),
        lax.psum_scatter(
            grad_w_turned.astype(jnp.bfloat16), "dp", scatter_dimension=0, tiled=True
        ).astype(jnp.float32),
    )
    summed = lax.psum(
        (bias_grad_full, grad_b_out, grad_gain_mix, grad_shift_mix, grad_gain_ffn, grad_shift_ffn),
        ("dp", "mp"),
    )
    return (
        jnp.concatenate(outputs, axis=0),
        jnp.concatenate(input_grads, axis=0),
        grad_w_in_part,
        summed[0],
        grad_w_turned_part.T,
        summed[1],
        summed[2],
        summed[3],
        summed[4],
        summed[5],
    )


def solution(mesh):
    return jax.shard_map(
        body,
        mesh=mesh,
        in_specs=(
            P(("dp", "mp"), None),
            P(("dp", "mp")),
            P("dp", "mp"),
            P("mp"),
            P("mp", "dp"),
            P(),
            P(),
            P(),
            P(),
            P(),
            P(("dp", "mp"), None),
        ),
        out_specs=(
            P(("dp", "mp"), None),
            P(("dp", "mp"), None),
            P("dp", "mp"),
            P(),
            P("mp", "dp"),
            P(),
            P(),
            P(),
            P(),
            P(),
        ),
        check_vma=False,
    )
```

profile of v0, /device:TPU:0, one launch (start us, length us, event | category | flops | bytes accessed | tf_op | source)
XLA Modules:
  0.0 1429.6 jit_solution(16443774621906451339)
XLA Ops:
  7.2 5.4 negate_convert_fusion
  12.6 10.7 multiply_convert_fusion.2
  23.3 0.6 fusion.60
  23.9 0.6 fusion.46
  24.6 0.7 fusion.45
  25.4 1.2 copy.55
  26.8 0.9 copy-done.17
  27.7 3.0 convolution_convert_fusion
  31.4 0.9 copy-done.18
  32.6 1.0 fusion.61
  34.1 0.9 copy-done.11
  35.0 2.6 convolution_convert_fusion.1
  37.6 3.6 reshape.228
  41.5 0.9 copy-done.16
  42.7 1.0 fusion.62
  44.4 1.6 fusion.25
  46.1 0.7 all-gather.7.cloned.1.call-update
  47.0 9.4 all_gather.21
  56.4 8.2 all_gather.22
  64.7 83.8 %all-gather.5.cloned.1.call-done = bf16[4096,768]{0,1:T(8,128)(2,1)} async-done(((bf16[512,768]{0,1:T(8,128)(2,1)}), bf16[4096,768]{0,1:T(8,128)(2,1)}) %all-gather.5.cloned.1.call-update) | async-done | bytes 6291472 | tf_op jit(solution)/shard_map/all_gather | solution.py:92
  148.5 5.9 convolution_add_fusion.1
  154.3 2.7 copy-done.36
  157.1 6.6 fusion.51
  163.7 85.1 %all-gather.7.cloned.1.call-done = bf16[4096,768]{0,1:T(8,128)(2,1)} async-done(((bf16[512,768]{0,1:T(8,128)(2,1)}), bf16[4096,768]{0,1:T(8,128)(2,1)}) %all-gather.7.cloned.1.call-update) | async-done | bytes 6291472 | tf_op jit(solution)/shard_map/all_gather | solution.py:92
  248.8 5.9 convolution_add_fusion
  254.7 2.6 copy-done.37
  257.3 6.5 fusion.49
  263.8 2.6 fusion.58
  266.4 2.4 copy.58
  268.8 2.3 copy.57
  271.1 1.3 fusion.39
  272.4 186.1 %reduce-scatter.7.cloned.1.call-done = f32[512,768]{0,1:T(8,128)} async-done(((f32[4096,768]{0,1:T(8,128)}), f32[512,768]{0,1:T(8,128)}) %reduce-scatter.7.cloned.1.call-update) | async-done | bytes 1572880 | tf_op jit(solution)/shard_map/reduce_scatter | solution.py:99
  458.5 210.5 %reduce-scatter.9.cloned.1.call-done = f32[512,768]{0,1:T(8,128)} async-done(((f32[4096,768]{0,1:T(8,128)}), f32[512,768]{0,1:T(8,128)}) %reduce-scatter.9.cloned.1.call-update) | async-done | bytes 1572880 | tf_op jit(solution)/shard_map/reduce_scatter | solution.py:99
  668.9 2.8 fusion.57
  671.8 1.1 multiply_reduce_fusion.7
  672.9 0.8 multiply_reduce_fusion.1
  673.8 1.5 convert_reduce_fusion.3
  675.4 3.2 convert_reduce_fusion.2
  678.8 95.2 %all-gather.9.cloned.1.call-done = bf16[4096,768]{0,1:T(8,128)(2,1)} async-done(((bf16[512,768]{0,1:T(8,128)(2,1)}), bf16[4096,768]{0,1:T(8,128)(2,1)}) %all-gather.9.cloned.1.call-update) | async-done | bytes 6291472 | tf_op jit(solution)/shard_map/all_gather | solution.py:111
  774.0 11.4 convert_reduce_fusion.1
  785.4 88.2 %all-gather.11.cloned.1.call-done = bf16[4096,768]{0,1:T(8,128)(2,1)} async-done(((bf16[512,768]{0,1:T(8,128)(2,1)}), bf16[4096,768]{0,1:T(8,128)(2,1)}) %all-gather.11.cloned.1.call-update) | async-done | bytes 6291472 | tf_op jit(solution)/shard_map/all_gather | solution.py:111
  873.6 10.4 convert_reduce_fusion
  884.1 6.7 fusion.65
  890.7 6.5 fusion.23
  897.7 8.2 fusion.50
  905.9 9.0 fusion.24
  915.0 10.0 fusion.64
  925.2 10.1 fusion.63
  935.5 1.6 convert_element_type.192
  937.2 5.1 reduce-scatter.17.cloned.1.call-done
  942.2 1.6 convert_bitcast_fusion
  943.9 209.8 %reduce-scatter.13.cloned.1.call-done = f32[512,768]{0,1:T(8,128)} async-done(((f32[4096,768]{0,1:T(8,128)}), f32[512,768]{0,1:T(8,128)}) %reduce-scatter.13.cloned.1.call-update) | async-done | bytes 1572880 | tf_op jit(solution)/shard_map/reduce_scatter | solution.py:117
  1153.7 4.0 multiply_reduce_fusion.2
  1157.7 206.4 %reduce-scatter.11.cloned.1.call-done = f32[512,768]{0,1:T(8,128)} async-done(((f32[4096,768]{0,1:T(8,128)}), f32[512,768]{0,1:T(8,128)}) %reduce-scatter.11.cloned.1.call-update) | async-done | bytes 1572880 | tf_op jit(solution)/shard_map/reduce_scatter | solution.py:117
  1364.1 3.3 multiply_reduce_fusion.3
  1367.4 2.6 fusion.54
  1370.2 1.6 copy.47
  1371.8 2.7 convolution_convert_fusion.2
  1374.7 1.3 copy-done.10
  1376.3 1.4 multiply_convert_fusion.4
  1377.9 1.0 convolution_convert_fusion.3
  1379.1 1.4 multiply_convert_fusion.5
  1380.7 1.6 copy.48
  1382.3 40.3 %all-reduce = (f32[3072]{0:T(1024)}, f32[768]{0:T(1024)}, f32[768]{0:T(1024)}, f32[768]{0:T(1024)}, f32[768]{0:T(1024)}, /*index=5*/f32[768]{0:T(1024)}) all-reduce(f32[3072]{0:T(1024)S(1)} %add_dynamic-update-slice_fusion, f32[768]{0:T(1024)S(1)} %add.235, f32[768]{0:T(1024)S(1)} %add.236, ...), channel_id=1, replica_groups=mesh['dp'=4,'mp'=8] {'dp','mp'}, use_global_device_ids=true, to_apply=%region_23.24 | all-reduce | flops 6912 | bytes 55296 | tf_op jit(solution)/shard_map/psum | solution.py:142
  (122 shorter events, 5.9 us)
Async XLA Ops:
  7.2 16.2 %copy-start.34 = (s32[2]{0:T(128)S(1)}, s32[2]{0:T(128)}, u32[]{:S(2)}) copy-start(s32[2]{0:T(128)} %param.12) | copy-start | bytes 28
  7.2 18.1 %copy-start.8 = (bf16[1024,768]{1,0:T(8,128)(2,1)S(1)}, bf16[1024,768]{1,0:T(8,128)(2,1)}, u32[]{:S(2)}) copy-start(bf16[1024,768]{1,0:T(8,128)(2,1)} %param.11) | copy-start | bytes 4718596
  7.2 141.3 %all-gather.5.cloned.1.call-start = ((), (), s32[]{:S(2)}) async-start(), calls=%async_computation.6 | async-start | bytes 7077888 | tf_op jit(solution)/shard_map/all_gather | solution.py:92
  26.8 0.9 copy-start.17
  31.1 1.1 copy-start.18
  31.2 1.3 copy-start.21
  31.2 1.4 copy-start.24
  32.6 1.3 copy-start.13
  32.6 1.5 copy-start.15
  33.6 1.4 copy-start.11
  41.2 1.1 copy-start.16
  41.2 1.3 copy-start.22
  41.3 1.4 copy-start.25
  43.7 0.7 copy-start.30
  43.7 0.7 copy-start.32
  46.1 0.8 copy-start.35
  46.1 0.9 copy-start.28
  46.1 10.4 copy-start.29
  46.1 202.7 %all-gather.7.cloned.1.call-start = ((), (), s32[]{:S(2)}) async-start(), calls=%async_computation.8 | async-start | bytes 7077888 | tf_op jit(solution)/shard_map/all_gather | solution.py:92
  46.9 411.6 %reduce-scatter.7.cloned.1.call-start = ((), (), s32[]{:S(2)}) async-start(), calls=%async_computation.7 | async-start | bytes 14155776 | tf_op jit(solution)/shard_map/reduce_scatter | solution.py:99
  148.5 8.6 copy-start.19
  154.3 2.7 copy-start.36
  163.7 505.3 %reduce-scatter.9.cloned.1.call-start = ((), (), s32[]{:S(2)}) async-start(), calls=%async_computation.9 | async-start | bytes 14155776 | tf_op jit(solution)/shard_map/reduce_scatter | solution.py:99
  248.8 8.5 copy-start.20
  254.7 2.6 copy-start.37
  263.8 510.3 %all-gather.9.cloned.1.call-start = ((), (), s32[]{:S(2)}) async-start(), calls=%async_computation.10 | async-start | bytes 7077888 | tf_op jit(solution)/shard_map/all_gather | solution.py:111
  266.4 402.5 %copy-start.33 = (f32[768]{0:T(1024)S(1)}, f32[768]{0:T(1024)}, u32[]{:S(2)}) copy-start(f32[768]{0:T(1024)} %param.16) | copy-start | bytes 9220
  272.4 399.4 %copy-start.27 = (f32[768]{0:T(1024)S(1)}, f32[768]{0:T(1024)}, u32[]{:S(2)}) copy-start(f32[768]{0:T(1024)} %param.19) | copy-start | bytes 9220
  668.9 2.9 copy-start.2
  668.9 2.9 copy-start.3
  671.8 2.0 copy-start
  671.8 2.0 copy-start.1
  675.3 198.3 %all-gather.11.cloned.1.call-start = ((), (), s32[]{:S(2)}) async-start(), calls=%async_computation.12 | async-start | bytes 7077888 | tf_op jit(solution)/shard_map/all_gather | solution.py:111
  678.5 257.0 %reduce-scatter.15.cloned.1.call-start = ((), (), s32[]{:S(2)}) async-start(), calls=%async_computation.14 | async-start | bytes 737280 | tf_op jit(solution)/shard_map/reduce_scatter | solution.py:135
  873.6 10.4 copy-start.5
  884.0 6.7 copy-start.6
  897.2 45.0 %reduce-scatter.17.cloned.1.call-start = ((), (), s32[]{:S(2)}) async-start(), calls=%async_computation.15 | async-start | bytes 737280 | tf_op jit(solution)/shard_map/reduce_scatter | solution.py:138
  914.9 238.8 %reduce-scatter.13.cloned.1.call-start = ((), (), s32[]{:S(2)}) async-start(), calls=%async_computation.13 | async-start | bytes 14155776 | tf_op jit(solution)/shard_map/reduce_scatter | solution.py:117
  925.0 439.1 %reduce-scatter.11.cloned.1.call-start = ((), (), s32[]{:S(2)}) async-start(), calls=%async_computation.11 | async-start | bytes 14155776 | tf_op jit(solution)/shard_map/reduce_scatter | solution.py:117
  935.3 218.4 %copy-start.31 = (f32[768]{0:T(1024)S(1)}, f32[768]{0:T(1024)}, u32[]{:S(2)}) copy-start(f32[768]{0:T(1024)} %param.20) | copy-start | bytes 9220
  1364.1 3.3 copy-start.4
  1367.4 2.6 copy-start.7
  1371.8 2.9 copy-start.14
  1374.5 1.4 copy-start.10
  1374.5 1.7 copy-start.12
  1376.3 1.4 copy-start.9
  1376.3 1.5 copy-start.23
  1376.3 1.7 copy-start.26
Sparse Core Ops, SparseCore 0:
  46.2 102.1 all-gather.4
  151.1 97.6 all-gather.6
  252.4 206.0 reduce-scatter.6
  461.9 206.9 reduce-scatter.8
  675.4 98.5 all-gather.8
  775.9 97.6 all-gather.10
  897.3 20.2 reduce-scatter.14
  920.1 22.0 reduce-scatter.16
  945.8 207.8 reduce-scatter.12
  1157.1 206.9 reduce-scatter.10
where the time goes:
time: 1440 us; the launch traced here: 1430 us
  waiting for transfers between devices  1170 us (81%)
  matrix products  111 us (8%)
  blocking collectives  58 us (4%)
  other arithmetic  44 us (3%)
  local copies, waits for them, and re-layouts  29.4 us (2%)
  between operations  14.9 us (1%)
    reduce_scatter x2, waiting for transfers between devices, body(): lax.psum_scatter(inner_rows(grad_pre, w_in_rows), 'mp', scatter_dimension...  416 us
    reduce_scatter x2, waiting for transfers between devices, body(): lax.psum_scatter(inner_rows(hidden, w_out_rows), 'mp', scatter_dimension=...  397 us
    all_gather x2, waiting for transfers between devices, body(): grad_gathered = lax.all_gather(grad_branch, 'mp', axis=0, tiled=True)  183 us
    all_gather x2, waiting for transfers between devices, body(): gathered = lax.all_gather(first_low, 'mp', axis=0, tiled=True)  169 us
    psum x1, blocking collectives, body(): lax.psum((bias_grad_full, grad_b_out, grad_gain_mix, grad_shift_mix, grad...  40.3 us
    dot_general x6, matrix products, inner_rows(): lax.dot_general(left, right, (((1,), (1,)), ((), ())), preferred_element_...  35.9 us
    dot_general x4, matrix products, outer_rows(): lax.dot_general(left, right, (((0,), (0,)), ((), ())), preferred_element_...  30.3 us
  transfers between devices with their start and end apart: 10, of which 9 were waited for; matrix products, arithmetic and copies ran while one was open for 6% of the time, Pallas kernels for 0%

commit v1 on v0

--- a/solution.py
+++ b/solution.py
@@ -1,3 +1,4 @@
+import functools
 from functools import partial
 import math
 import jax
@@ -11,6 +12,23 @@
 MB = 2
 SEQ_MB = 1
 epsilon = 1e-06
+
+
+def balance_the_steps_all(local_values, join_dim):
+    m_next = lax.axis_size("mp")
+    aux = lax.axis_index("mp")
+    r2, block_last = (m_next, aux)
+    prior, fresh = (local_values, 1)
+    while fresh < r2:
+        t1 = lax.ppermute(prior, axis_name="mp", perm=[(h, h ^ fresh) for h in range(r2)])
+        x_new = jnp.concatenate([prior, t1], join_dim)
+        local_part = jnp.concatenate([t1, prior], join_dim)
+        prior = jnp.where(block_last & fresh == 0, x_new, local_part)
+        fresh = 2 * fresh
+    return prior
+
+
+_bring_area = functools.partial(balance_the_steps_all, join_dim=0)
 
 
 def dft_tables(width):
@@ -89,7 +107,7 @@
             lax.all_gather(w_in, "dp", axis=0, tiled=True),
             lax.all_gather(w_out_turned, "dp", axis=0, tiled=True),
         )
-        gathered = lax.all_gather(first_low, "mp", axis=0, tiled=True)
+        gathered = _bring_area(first_low)
         pre_act = jnp.dot(gathered, w_in_rows, preferred_element_type=jnp.float32) + b_in.astype(
             jnp.float32
         )

time: 1440 us -> 1590 us (1.10)
  waiting for transfers between devices: 1170 us -> 1300 us
    ppermute x0 -> x6, waiting for transfers between devices: none -> 496 us  [balance_the_steps_all(): lax.ppermute(prior, axis_name='mp', perm=[(h, h ^ fresh) for h in range(r...]
    reduce_scatter x2, waiting for transfers between devices: 397 us -> 200 us  [body(): lax.psum_scatter(inner_rows(hidden, w_out_rows), 'mp', scatter_dimension=...]
    all_gather x2 -> x0, waiting for transfers between devices: 169 us -> none  [body(): gathered = lax.all_gather(first_low, 'mp', axis=0, tiled=True)]
  transfers between devices with their start and end apart: 10 -> 14, of which waited for: 9 -> 12; matrix products, arithmetic and copies ran while one was open for 6% -> 5% of each run, Pallas kernels for 0% -> 0%
where the time goes in v1:
time: 1590 us; the launch traced here: 1580 us
  waiting for transfers between devices  1300 us (82%)
  matrix products  111 us (7%)
  other arithmetic  56.3 us (4%)
  blocking collectives  55.8 us (4%)
  local copies, waits for them, and re-layouts  28.1 us (2%)
    ppermute x6, waiting for transfers between devices, balance_the_steps_all(): lax.ppermute(prior, axis_name='mp', perm=[(h, h ^ fresh) for h in range(r...  496 us
    reduce_scatter x2, waiting for transfers between devices, body(): lax.psum_scatter(inner_rows(grad_pre, w_in_rows), 'mp', scatter_dimension...  416 us
    reduce_scatter x2, waiting for transfers between devices, body(): lax.psum_scatter(inner_rows(hidden, w_out_rows), 'mp', scatter_dimension=...  200 us
    all_gather x2, waiting for transfers between devices, body(): grad_gathered = lax.all_gather(grad_branch, 'mp', axis=0, tiled=True)  183 us
    psum x1, blocking collectives, body(): lax.psum((bias_grad_full, grad_b_out, grad_gain_mix, grad_shift_mix, grad...  40.3 us
    dot_general x6, matrix products, inner_rows(): lax.dot_general(left, right, (((1,), (1,)), ((), ())), preferred_element_...  35.9 us
  transfers between devices with their start and end apart: 14, of which 12 were waited for; matrix products, arithmetic and copies ran while one was open for 5% of the time, Pallas kernels for 0%

profile of v1, /device:TPU:0, one launch (start us, length us, event | category | flops | bytes accessed | tf_op | source)
XLA Modules:
  0.0 1577.1 jit_solution(5815085761014625078)
XLA Ops:
  7.2 5.4 negate_convert_fusion
  12.6 10.7 multiply_convert_fusion.2
  25.4 1.2 copy.55
  27.7 3.0 convolution_convert_fusion
  32.6 1.0 fusion.66
  34.4 2.6 convolution_convert_fusion.1
  37.0 3.6 reshape.228
  43.4 1.7 fusion.25
  45.1 3.0 collective-permute-start
  48.1 17.9 %collective-permute-done = bf16[512,768]{0,1:T(8,128)(2,1)} collective-permute-done((bf16[512,768]{0,1:T(8,128)(2,1)}, bf16[512,768]{0,1:T(8,128)(2,1)}, u32[]{:S(2)}, u32[]{:S(2)}) %collective-permute-start) | collective-permute-done | bytes 786464 | tf_op jit(solution)/shard_map/ppermute | solution.py:23
  65.9 3.7 maximum_select_fusion.4
  69.6 1.8 collective-permute-start.1
  71.4 34.1 %collective-permute-done.1 = bf16[1024,768]{0,1:T(8,128)(2,1)} collective-permute-done((bf16[1024,768]{0,1:T(8,128)(2,1)}, bf16[1024,768]{0,1:T(8,128)(2,1)}, u32[]{:S(2)}, u32[]{:S(2)}) %collective-permute-start.1) | collective-permute-done | bytes 1572896 | tf_op jit(solution)/shard_map/ppermute | solution.py:23
  105.5 5.5 maximum_select_fusion.2
  111.0 2.5 collective-permute-start.2
  113.5 7.5 all_gather.14
  121.1 8.0 all_gather.15
  129.0 119.0 %collective-permute-done.2 = bf16[2048,768]{0,1:T(8,128)(2,1)} collective-permute-done((bf16[2048,768]{0,1:T(8,128)(2,1)}, bf16[2048,768]{0,1:T(8,128)(2,1)}, u32[]{:S(2)}, u32[]{:S(2)}) %collective-permute-start.2) | collective-permute-done | bytes 3145760 | tf_op jit(solution)/shard_map/ppermute | solution.py:23
  248.0 8.5 convolution_add_fusion.1
  256.6 2.6 copy-done.46
  259.2 6.6 fusion.56
  265.8 1.2 collective-permute-start.3
  267.1 28.4 %collective-permute-done.3 = bf16[512,768]{0,1:T(8,128)(2,1)S(1)} collective-permute-done((bf16[512,768]{0,1:T(8,128)(2,1)}, bf16[512,768]{0,1:T(8,128)(2,1)S(1)}, u32[]{:S(2)}, u32[]{:S(2)}) %collective-permute-start.3) | collective-permute-done | bytes 786464 | tf_op jit(solution)/shard_map/ppermute | solution.py:23
  295.5 1.9 maximum_select_fusion.5
  297.5 108.5 %collective-permute-done.4 = bf16[1024,768]{0,1:T(8,128)(2,1)S(1)} collective-permute-done((bf16[1024,768]{0,1:T(8,128)(2,1)S(1)}, bf16[1024,768]{0,1:T(8,128)(2,1)S(1)}, u32[]{:S(2)}, u32[]{:S(2)}) %collective-permute-start.4) | collective-permute-done | bytes 1572896 | tf_op jit(solution)/shard_map/ppermute | solution.py:23
  406.1 1.2 maximum_select_fusion.3
  407.4 187.9 %collective-permute-done.5 = bf16[2048,768]{0,1:T(8,128)(2,1)S(1)} collective-permute-done((bf16[2048,768]{0,1:T(8,128)(2,1)S(1)}, bf16[2048,768]{0,1:T(8,128)(2,1)S(1)}, u32[]{:S(2)}, u32[]{:S(2)}) %collective-permute-start.5) | collective-permute-done | bytes 3145760 | tf_op jit(solution)/shard_map/ppermute | solution.py:23
  595.2 3.5 convolution_add_fusion
  598.8 2.6 copy-done.47
  601.4 6.5 fusion.54
  608.0 2.6 fusion.63
  610.6 2.3 copy.58
  612.9 2.3 copy.57
  615.2 1.3 fusion.40
  616.6 200.0 %reduce-scatter.9.cloned.1.call-done = f32[512,768]{0,1:T(8,128)} async-done(((f32[4096,768]{0,1:T(8,128)}), f32[512,768]{0,1:T(8,128)}) %reduce-scatter.9.cloned.1.call-update) | async-done | bytes 1572880 | tf_op jit(solution)/shard_map/reduce_scatter | solution.py:117
  816.6 2.8 fusion.62
  819.5 1.1 multiply_reduce_fusion.7
  821.5 1.5 convert_reduce_fusion.3
  823.2 3.1 convert_reduce_fusion.2
  826.4 95.3 %all-gather.3.cloned.1.call-done = bf16[4096,768]{0,1:T(8,128)(2,1)} async-done(((bf16[512,768]{0,1:T(8,128)(2,1)}), bf16[4096,768]{0,1:T(8,128)(2,1)}) %all-gather.3.cloned.1.call-update) | async-done | bytes 6291472 | tf_op jit(solution)/shard_map/all_gather | solution.py:129
  921.7 11.4 convert_reduce_fusion.1
  933.1 88.2 %all-gather.5.cloned.1.call-done = bf16[4096,768]{0,1:T(8,128)(2,1)} async-done(((bf16[512,768]{0,1:T(8,128)(2,1)}), bf16[4096,768]{0,1:T(8,128)(2,1)}) %all-gather.5.cloned.1.call-update) | async-done | bytes 6291472 | tf_op jit(solution)/shard_map/all_gather | solution.py:129
  1021.3 10.4 convert_reduce_fusion
  1031.8 3.8 fusion.27
  1035.6 9.5 fusion.23
  1045.3 8.2 fusion.55
  1053.6 9.0 fusion.24
  1062.7 9.9 fusion.68
  1073.0 10.1 fusion.69
  1083.3 1.6 convert_element_type.192
  1084.9 5.0 reduce-scatter.17.cloned.1.call-done
  1089.9 1.6 convert_bitcast_fusion
  1091.6 209.8 %reduce-scatter.11.cloned.1.call-done = f32[512,768]{0,1:T(8,128)} async-done(((f32[4096,768]{0,1:T(8,128)}), f32[512,768]{0,1:T(8,128)}) %reduce-scatter.11.cloned.1.call-update) | async-done | bytes 1572880 | tf_op jit(solution)/shard_map/reduce_scatter | solution.py:135
  1301.4 4.0 multiply_reduce_fusion.3
  1305.5 206.5 %reduce-scatter.13.cloned.1.call-done = f32[512,768]{0,1:T(8,128)} async-done(((f32[4096,768]{0,1:T(8,128)}), f32[512,768]{0,1:T(8,128)}) %reduce-scatter.13.cloned.1.call-update) | async-done | bytes 1572880 | tf_op jit(solution)/shard_map/reduce_scatter | solution.py:135
  1512.0 3.3 multiply_reduce_fusion.2
  1515.4 2.6 fusion.59
  1518.1 1.6 copy.47
  1519.7 2.2 convolution_convert_fusion.2
  1522.0 1.1 copy-done.16
  1523.5 1.4 multiply_convert_fusion.4
  1526.3 1.4 multiply_convert_fusion.5
  1527.9 1.6 copy.48
  1529.5 40.3 %all-reduce = (f32[3072]{0:T(1024)}, f32[768]{0:T(1024)}, f32[768]{0:T(1024)}, f32[768]{0:T(1024)}, f32[768]{0:T(1024)}, /*index=5*/f32[768]{0:T(1024)}) all-reduce(f32[3072]{0:T(1024)S(1)} %add_dynamic-update-slice_fusion, f32[768]{0:T(1024)S(1)} %add.235, f32[768]{0:T(1024)S(1)} %add.236, ...), channel_id=1, replica_groups=mesh['dp'=4,'mp'=8] {'dp','mp'}, use_global_device_ids=true, to_apply=%region_23.24 | all-reduce | flops 6912 | bytes 55296 | tf_op jit(solution)/shard_map/psum | solution.py:160
  (152 shorter events, 13.1 us)
Async XLA Ops:
  7.2 16.2 %copy-start.42 = (s32[2]{0:T(128)S(1)}, s32[2]{0:T(128)}, u32[]{:S(2)}) copy-start(s32[2]{0:T(128)} %param.12) | copy-start | bytes 28
  7.2 18.1 %copy-start.12 = (bf16[1024,768]{1,0:T(8,128)(2,1)S(1)}, bf16[1024,768]{1,0:T(8,128)(2,1)}, u32[]{:S(2)}) copy-start(bf16[1024,768]{1,0:T(8,128)(2,1)} %param.11) | copy-start | bytes 4718596
  7.2 609.4 %reduce-scatter.7.cloned.1.call-start = ((), (), s32[]{:S(2)}) async-start(), calls=%async_computation.6 | async-start | bytes 14155776 | tf_op jit(solution)/shard_map/reduce_scatter | solution.py:117
  26.8 0.9 copy-start.21
  31.1 1.1 copy-start.22
  31.2 1.3 copy-start.25
  31.2 1.4 copy-start.28
  32.6 1.3 copy-start.15
  32.6 1.6 copy-start.17
  32.6 1.8 copy-start.19
  33.9 3.1 copy-start.35
  40.6 1.1 copy-start.20
  40.7 1.3 copy-start.26
  40.7 1.4 copy-start.29
  42.1 1.3 copy-start.34
  42.1 1.3 copy-start.40
  43.4 1.7 copy-start.37
  45.1 20.8 %collective-permute-start = (bf16[512,768]{0,1:T(8,128)(2,1)}, bf16[512,768]{0,1:T(8,128)(2,1)}, u32[]{:S(2)}, u32[]{:S(2)}) collective-permute-start(bf16[512,768]{0,1:T(8,128)(2,1)} %get-tuple-element.81), channel_id=1, source_target_pairs={{0,1},{1,0},{2,3},{3,2},{4,5},{5,4},{6,7},{7,6},{8,9},{9,8},{10,11... | collective-permute-start | bytes 2359304 | tf_op jit(solution)/shard_map/ppermute | solution.py:23
  69.6 35.9 %collective-permute-start.1 = (bf16[1024,768]{0,1:T(8,128)(2,1)}, bf16[1024,768]{0,1:T(8,128)(2,1)}, u32[]{:S(2)}, u32[]{:S(2)}) collective-permute-start(bf16[1024,768]{0,1:T(8,128)(2,1)} %maximum_select_fusion.4), channel_id=1, source_target_pairs={{0,2},{1,3},{2,0},{3,1},{4,6},{5,7},{6,4},{7,5},{8,10},{9,11},{10,... | collective-permute-start | bytes 4718600 | tf_op jit(solution)/shard_map/ppermute | solution.py:23
  71.4 42.1 %copy-start.43 = (bf16[384]{0:T(512)(128)(2,1)S(1)}, bf16[384]{0:T(512)(128)(2,1)}, u32[]{:S(2)}) copy-start(bf16[384]{0:T(512)(128)(2,1)} %param.14) | copy-start | bytes 2308
  71.4 42.1 %copy-start.32 = (bf16[192,384]{1,0:T(8,128)(2,1)S(1)}, bf16[192,384]{1,0:T(8,128)(2,1)}, u32[]{:S(2)}) copy-start(bf16[192,384]{1,0:T(8,128)(2,1)} %param.13) | copy-start | bytes 442372
  71.4 49.6 %copy-start.33 = (bf16[384,192]{0,1:T(8,128)(2,1)S(1)}, bf16[384,192]{0,1:T(8,128)(2,1)}, u32[]{:S(2)}) copy-start(bf16[384,192]{0,1:T(8,128)(2,1)} %param.15) | copy-start | bytes 442372
  111.0 137.0 %collective-permute-start.2 = (bf16[2048,768]{0,1:T(8,128)(2,1)}, bf16[2048,768]{0,1:T(8,128)(2,1)}, u32[]{:S(2)}, u32[]{:S(2)}) collective-permute-start(bf16[2048,768]{0,1:T(8,128)(2,1)} %maximum_select_fusion.2), channel_id=1, source_target_pairs={{0,4},{1,5},{2,6},{3,7},{4,0},{5,1},{6,2},{7,3},{8,12},{9,13},{10,... | collective-permute-start | bytes 9437192 | tf_op jit(solution)/shard_map/ppermute | solution.py:23
  121.1 135.5 %copy-start.7 = (bf16[768,384]{1,0:T(8,128)(2,1)}, bf16[768,384]{1,0:T(8,128)(2,1)S(1)}, u32[]{:S(2)}) copy-start(bf16[768,384]{1,0:T(8,128)(2,1)S(1)} %all_gather.14) | copy-start | bytes 1769476
  129.0 127.5 %copy-start.23 = (bf16[768,384]{1,0:T(8,128)(2,1)}, bf16[768,384]{1,0:T(8,128)(2,1)S(1)}, u32[]{:S(2)}) copy-start(bf16[768,384]{1,0:T(8,128)(2,1)S(1)} %all_gather.15) | copy-start | bytes 1769476
  256.5 2.6 copy-start.46
  265.8 550.8 %reduce-scatter.9.cloned.1.call-start = ((), (), s32[]{:S(2)}) async-start(), calls=%async_computation.7 | async-start | bytes 14155776 | tf_op jit(solution)/shard_map/reduce_scatter | solution.py:117
  265.8 29.7 %collective-permute-start.3 = (bf16[512,768]{0,1:T(8,128)(2,1)}, bf16[512,768]{0,1:T(8,128)(2,1)S(1)}, u32[]{:S(2)}, u32[]{:S(2)}) collective-permute-start(bf16[512,768]{0,1:T(8,128)(2,1)} %get-tuple-element.82), channel_id=1, source_target_pairs={{0,1},{1,0},{2,3},{3,2},{4,5},{5,4},{6,7},{7,6},{8,9},{9,8},{10,11... | collective-permute-start | bytes 2359304 | tf_op jit(solution)/shard_map/ppermute | solution.py:23
  297.4 297.8 %copy-start.8 = (bf16[768,384]{1,0:T(8,128)(2,1)S(1)}, bf16[768,384]{1,0:T(8,128)(2,1)}, u32[]{:S(2)}) copy-start(bf16[768,384]{1,0:T(8,128)(2,1)} %copy-done.7) | copy-start | bytes 1769476
  297.4 108.7 %collective-permute-start.4 = (bf16[1024,768]{0,1:T(8,128)(2,1)S(1)}, bf16[1024,768]{0,1:T(8,128)(2,1)S(1)}, u32[]{:S(2)}, u32[]{:S(2)}) collective-permute-start(bf16[1024,768]{0,1:T(8,128)(2,1)S(1)} %maximum_select_fusion.5), channel_id=1, source_target_pairs={{0,2},{1,3},{2,0},{3,1},{4,6},{5,7},{6,4},{7,5},{8,10},{9,11},{10,... | collective-permute-start | bytes 4718600 | tf_op jit(solution)/shard_map/ppermute | solution.py:23
  407.3 191.5 %copy-start.9 = (bf16[2048,768]{0,1:T(8,128)(2,1)}, bf16[2048,768]{0,1:T(8,128)(2,1)S(1)}, u32[]{:S(2)}) copy-start(bf16[2048,768]{0,1:T(8,128)(2,1)S(1)} %maximum_select_fusion.3) | copy-start | bytes 9437188
  407.3 194.1 %copy-start.24 = (bf16[768,384]{1,0:T(8,128)(2,1)S(1)}, bf16[768,384]{1,0:T(8,128)(2,1)}, u32[]{:S(2)}) copy-start(bf16[768,384]{1,0:T(8,128)(2,1)} %copy-done.23) | copy-start | bytes 1769476
  407.3 187.9 %collective-permute-start.5 = (bf16[2048,768]{0,1:T(8,128)(2,1)S(1)}, bf16[2048,768]{0,1:T(8,128)(2,1)S(1)}, u32[]{:S(2)}, u32[]{:S(2)}) collective-permute-start(bf16[2048,768]{0,1:T(8,128)(2,1)S(1)} %maximum_select_fusion.3), channel_id=1, source_target_pairs={{0,4},{1,5},{2,6},{3,7},{4,0},{5,1},{6,2},{7,3},{8,12},{9,13},{10,... | collective-permute-start | bytes 9437192 | tf_op jit(solution)/shard_map/ppermute | solution.py:23
  595.2 3.6 copy-start.44
  598.8 2.6 copy-start.47
  607.9 313.8 %all-gather.3.cloned.1.call-start = ((), (), s32[]{:S(2)}) async-start(), calls=%async_computation.8 | async-start | bytes 7077888 | tf_op jit(solution)/shard_map/all_gather | solution.py:129
  610.6 206.0 %copy-start.41 = (f32[768]{0:T(1024)S(1)}, f32[768]{0:T(1024)}, u32[]{:S(2)}) copy-start(f32[768]{0:T(1024)} %param.16) | copy-start | bytes 9220
  616.6 203.0 %copy-start.31 = (f32[768]{0:T(1024)S(1)}, f32[768]{0:T(1024)}, u32[]{:S(2)}) copy-start(f32[768]{0:T(1024)} %param.19) | copy-start | bytes 9220
  816.6 2.9 copy-start.2
  816.6 2.9 copy-start.3
  819.5 2.0 copy-start
  819.5 2.0 copy-start.1
  823.0 198.3 %all-gather.5.cloned.1.call-start = ((), (), s32[]{:S(2)}) async-start(), calls=%async_computation.10 | async-start | bytes 7077888 | tf_op jit(solution)/shard_map/all_gather | solution.py:129
  826.4 256.9 %reduce-scatter.15.cloned.1.call-start = ((), (), s32[]{:S(2)}) async-start(), calls=%async_computation.12 | async-start | bytes 737280 | tf_op jit(solution)/shard_map/reduce_scatter | solution.py:153
  1021.3 10.4 copy-start.10
  1021.3 10.4 copy-start.45
  1031.7 3.8 copy-start.5
  1031.8 3.8 copy-start.6
  1045.1 44.8 %reduce-scatter.17.cloned.1.call-start = ((), (), s32[]{:S(2)}) async-start(), calls=%async_computation.13 | async-start | bytes 737280 | tf_op jit(solution)/shard_map/reduce_scatter | solution.py:156
  1062.6 238.8 %reduce-scatter.11.cloned.1.call-start = ((), (), s32[]{:S(2)}) async-start(), calls=%async_computation.9 | async-start | bytes 14155776 | tf_op jit(solution)/shard_map/reduce_scatter | solution.py:135
  1072.7 439.3 %reduce-scatter.13.cloned.1.call-start = ((), (), s32[]{:S(2)}) async-start(), calls=%async_computation.11 | async-start | bytes 14155776 | tf_op jit(solution)/shard_map/reduce_scatter | solution.py:135
  1083.1 218.4 %copy-start.39 = (f32[768]{0:T(1024)S(1)}, f32[768]{0:T(1024)}, u32[]{:S(2)}) copy-start(f32[768]{0:T(1024)} %param.20) | copy-start | bytes 9220
  1091.6 213.9 %copy-start.38 = (f32[512]{0:T(512)S(1)}, f32[512]{0:T(512)}, u32[]{:S(2)}) copy-start(f32[512]{0:T(512)} %copy-done.37) | copy-start | bytes 6148
  1305.4 209.9 %copy-start.36 = (f32[512]{0:T(512)S(1)}, f32[512]{0:T(512)}, u32[]{:S(2)}) copy-start(f32[512]{0:T(512)} %copy-done.35) | copy-start | bytes 6148
  1512.0 3.4 copy-start.4
  1515.4 2.6 copy-start.11
  1518.1 1.6 copy-start.14
  1521.9 1.3 copy-start.16
  1521.9 1.6 copy-start.18
  1523.5 1.4 copy-start.13
  1523.5 1.5 copy-start.27
  1523.5 1.7 copy-start.30
Sparse Core Ops, SparseCore 0:
  265.9 292.0 reduce-scatter.6
  608.1 208.5 reduce-scatter.8
  823.1 98.5 all-gather.2
  923.6 97.6 all-gather.4
  1045.2 20.2 reduce-scatter.14
  1067.8 22.0 reduce-scatter.16
  1093.5 207.8 reduce-scatter.10
  1305.0 206.9 reduce-scatter.12
